TPU v7x, 512 devices: a whole 4x8x8 slice. The times are simulated.
512 devices in a mesh: row: 32 (over z, y_lo), col: 4 (over y_hi, core), head: 4 (over x).
Axes of the slice: x: 4, y: 8 (y_hi: 2, y_lo: 4; y = y_hi * 4 + y_lo), z: 8, core: 2. Of those that a mesh axis runs over, the one named last changes fastest.
Arguments:
- tokens: bfloat16 [512, 128, 1024], P(('row', 'head'), 'col'), may hold values from -6 to 6
- valid: int32 [512, 128], P('row', 'col'), may hold values 0 or 1
- gain: float32 [1024], replicated, may hold values from 0.1 to 1.9
- w_qkv: bfloat16 [1024, 3, 1024], P(None, None, 'head'), may hold values from -0.1875 to 0.1875
- w_proj: bfloat16 [1024, 1024], P('head'), may hold values from -0.1875 to 0.1875
- rel_table: float32 [225, 16], P(None, 'head'), may hold values from -4 to 300
- cotangent: bfloat16 [512, 128, 1024], P(('row', 'head'), 'col'), may hold values from -24 to 24
Outputs:
- mixed: bfloat16 [512, 128, 1024], P(('row', 'head'), 'col')
- token_gradient: bfloat16 [512, 128, 1024], P(('row', 'head'), 'col')
- proj_grad: float32 [1024, 1024], P('head', ('row', 'col'))
- table_grad: float32 [225, 16], P(None, 'head')
All inputs are finite; a program needn't handle non-finite values. No bound on the sum of `valid` on one device may be relied on, other than what follows from the above.
Results may differ from a plain program's by a relative error of at most 0.0078.
Values may be sent and summed in bfloat16 or wider, within the bound.
No kernel may reach another device: no remote copies, remote signals or barrier semaphores. Data moves between devices by JAX's collectives and lax.ppermute only.
A program may use at most 64 MiB of HBM per device.

v0:
```python
import math
import jax
import jax.numpy as jnp
from jax import lax
from jax.sharding import PartitionSpec as P

HD = 64
WIN = 8
SHIFT = 4
EPS = 1e-05
HIGH = lax.Precision.HIGHEST


def passed_along(value, axis, steps):
    count = lax.axis_size(axis)
    pairs = [(source, (source + steps) % count) for source in range(count)]
    return lax.ppermute(value, axis, pairs)


def region(index, grand_total):
    return jnp.where(
        index < grand_total - WIN, 0, jnp.where(index < grand_total - SHIFT, 1, 2)
    ).astype(jnp.int32)


def offsets():
    span = 2 * WIN - 1
    pos = jnp.arange(WIN * WIN, dtype=jnp.int32)
    prow = pos // WIN
    pcol = pos % WIN
    index = (prow[:, None] - prow[None, :] + WIN - 1) * span + (
        pcol[:, None] - pcol[None, :] + WIN - 1
    )
    table_ids = jnp.arange(span * span, dtype=jnp.int32)
    return (
        (index[:, :, None] == table_ids[None, None, :])
        .astype(jnp.float32)
        .reshape(WIN * WIN * WIN * WIN, span * span)
    )


def to_windows(block):
    nrow, ncol, heads, depth = block.shape
    block = block.reshape(nrow // WIN, WIN, ncol // WIN, WIN, heads, depth).transpose(
        0, 2, 4, 1, 3, 5
    )
    return block.reshape(nrow // WIN * (ncol // WIN), heads, WIN * WIN, depth)


def from_windows(block, nrow, ncol):
    count, heads, posn, depth = block.shape
    block = block.reshape(nrow // WIN, ncol // WIN, heads, WIN, WIN, depth).transpose(
        0, 3, 1, 4, 2, 5
    )
    return block.reshape(nrow, ncol, heads * depth)


def rows_in(block):
    return jnp.concatenate([block[SHIFT:], passed_along(block[:SHIFT], "row", -1)], 0)


def cols_in(block):
    return jnp.concatenate([block[:, SHIFT:], passed_along(block[:, :SHIFT], "col", -1)], 1)


def rows_out(block):
    return jnp.concatenate([passed_along(block[-SHIFT:], "row", 1), block[:-SHIFT]], 0)


def cols_out(block):
    return jnp.concatenate([passed_along(block[:, -SHIFT:], "col", 1), block[:, :-SHIFT]], 1)


def roll_in(block):
    return cols_in(rows_in(block))


def roll_out(block):
    return cols_out(rows_out(block))


def roll_pair(first, second, roller):
    return (roller(first), roller(second))


def head_sum(term_fn, part_rows):
    return lax.psum_scatter(
        term_fn(jnp.int32(0), lax.axis_size("head") * part_rows).astype(jnp.bfloat16),
        "head",
        scatter_dimension=0,
        tiled=True,
    ).astype(jnp.float32)


def attend(qkv, grad, labels, valid, bias, onehot):
    nrow, ncol = labels.shape
    feature_width = qkv.shape[3]
    heads = feature_width // HD
    scale = HD ** (-0.5)
    f32 = jnp.float32
    query = to_windows(qkv[:, :, 0].reshape(nrow, ncol, heads, HD))
    key = to_windows(qkv[:, :, 1].reshape(nrow, ncol, heads, HD))
    value = to_windows(qkv[:, :, 2].reshape(nrow, ncol, heads, HD))
    dout = to_windows(grad.reshape(nrow, ncol, heads, HD))
    lab_win = to_windows(labels[:, :, None, None])[:, 0, :, 0]
    val_win = to_windows(valid[:, :, None, None])[:, 0, :, 0]
    diagonal = jnp.eye(WIN * WIN, dtype=bool)
    allowed = (lab_win[:, :, None] == lab_win[:, None, :]) & (
        (val_win[:, None, :] == 1) | diagonal[None]
    )
    scores = (
        jnp.einsum("wiqd,wikd->wiqk", query, key, preferred_element_type=f32) * scale + bias[None]
    )
    scores = jnp.where(allowed[:, None], scores, -1e30)
    top = jnp.max(scores, -1, keepdims=True)
    expo = jnp.exp(scores - top)
    prob = expo / jnp.sum(expo, -1, keepdims=True)
    prob_b = prob.astype(jnp.bfloat16)
    attended = jnp.einsum("wiqk,wikd->wiqd", prob_b, value, preferred_element_type=f32).astype(
        jnp.bfloat16
    )
    dprob = jnp.einsum("wiqd,wikd->wiqk", dout, value, preferred_element_type=f32)
    dvalue = jnp.einsum("wiqk,wiqd->wikd", prob_b, dout, preferred_element_type=f32).astype(
        jnp.bfloat16
    )
    dscore = prob * (dprob - jnp.sum(prob * dprob, -1, keepdims=True))
    dscore_b = dscore.astype(jnp.bfloat16)
    dquery = (
        jnp.einsum("wiqk,wikd->wiqd", dscore_b, key, preferred_element_type=f32) * scale
    ).astype(jnp.bfloat16)
    dkey = (
        jnp.einsum("wiqk,wiqd->wikd", dscore_b, query, preferred_element_type=f32) * scale
    ).astype(jnp.bfloat16)
    summed = jnp.sum(dscore, 0).transpose(1, 2, 0).reshape(WIN * WIN * WIN * WIN, heads)
    tgrad = jnp.dot(onehot.T, summed, precision=HIGH)
    grads = jnp.stack(
        [
            from_windows(dquery, nrow, ncol),
            from_windows(dkey, nrow, ncol),
            from_windows(dvalue, nrow, ncol),
        ],
        2,
    )
    return (from_windows(attended, nrow, ncol), grads, tgrad)


def on_device(tokens, valid, gain, w_qkv, w_proj, rel_table, cotangent):
    part_rows, ncol, feature_width = tokens.shape
    tile_rows = part_rows * lax.axis_size("head")
    row_count = lax.axis_size("row")
    col_count = lax.axis_size("col")
    flat = tokens.astype(jnp.float32)
    token_average = jnp.mean(flat, -1, keepdims=True)
    centered_input = flat - token_average
    inverse_deviation = lax.rsqrt(
        jnp.mean(centered_input * centered_input, -1, keepdims=True) + EPS
    )
    standardized_input = centered_input * inverse_deviation
    normalized_tokens = (standardized_input * gain).astype(jnp.bfloat16)
    grad_tile = lax.all_gather(cotangent, "head", axis=0, tiled=True)
    out_grad = jnp.einsum(
        "rcd,nd->rcn", grad_tile, w_proj, preferred_element_type=jnp.float32
    ).astype(jnp.bfloat16)
    source = lax.all_gather(normalized_tokens, "head", axis=0, tiled=True)
    moved, rolled_grad = roll_pair(source, out_grad, roll_in)
    rolled = jnp.einsum("rcd,dtn->rctn", moved, w_qkv, preferred_element_type=jnp.float32).astype(
        jnp.bfloat16
    )
    row_lab = region(
        lax.axis_index("row") * tile_rows + jnp.arange(tile_rows, dtype=jnp.int32),
        tile_rows * row_count,
    )
    col_lab = region(
        lax.axis_index("col") * ncol + jnp.arange(ncol, dtype=jnp.int32), ncol * col_count
    )
    labels = 3 * row_lab[:, None] + col_lab[None, :]
    onehot = offsets()
    heads = rel_table.shape[1]
    bias = (
        jnp.dot(onehot, rel_table, precision=HIGH)
        .reshape(WIN * WIN, WIN * WIN, heads)
        .transpose(2, 0, 1)
    )
    attended, grads, tgrad = attend(rolled, rolled_grad, labels, valid, bias, onehot)
    attn_out, qkv_grad = roll_pair(attended, grads, roll_out)

    def proj_term(start, count):
        return jnp.einsum("rcn,nd->rcd", attn_out, w_proj, preferred_element_type=jnp.float32)

    def back_term(start, count):
        return jnp.einsum("rctn,dtn->rcd", qkv_grad, w_qkv, preferred_element_type=jnp.float32)

    mixed = (flat + head_sum(proj_term, part_rows)).astype(jnp.bfloat16)
    norm_grad = head_sum(back_term, part_rows)
    scale = 1.0 / math.sqrt(tile_rows * ncol * row_count * col_count)
    weight_term = jnp.einsum("rcn,rcd->nd", attn_out, grad_tile, preferred_element_type=jnp.float32)
    proj_grad = (
        lax.psum_scatter(weight_term, ("row", "col"), scatter_dimension=1, tiled=True) * scale
    )
    table_grad = lax.psum(tgrad, ("row", "col")) * (WIN * scale)
    scaled_tokens = norm_grad * gain
    token_gradient = cotangent.astype(jnp.float32) + inverse_deviation * (
        scaled_tokens
        - jnp.mean(scaled_tokens, -1, keepdims=True)
        - standardized_input * jnp.mean(scaled_tokens * standardized_input, -1, keepdims=True)
    )
    return (mixed, token_gradient.astype(jnp.bfloat16), proj_grad, table_grad)


def solution(mesh):
    return jax.shard_map(
        on_device,
        mesh=mesh,
        in_specs=(
            P(("row", "head"), "col", None),
            P("row", "col"),
            P(),
            P(None, None, "head"),
            P("head", None),
            P(None, "head"),
            P(("row", "head"), "col", None),
        ),
        out_specs=(
            P(("row", "head"), "col", None),
            P(("row", "head"), "col", None),
            P("head", ("row", "col")),
            P(None, "head"),
        ),
        check_vma=False,
    )
```

profile of v0, /device:TPU:8, one launch (start us, length us, event | category | flops | bytes accessed | tf_op | source)
XLA Modules:
  0.0 753.7 jit_solution(1386446947580851297)
XLA Ops:
  7.2 1.2 convert_reduce_fusion
  8.5 1.2 fusion.36
  10.2 1.9 fusion.30
  14.0 3.4 fusion.17
  17.5 28.7 %all-gather.3.cloned.1.call-done = bf16[16,32,1024]{2,1,0:T(8,128)(2,1)} async-done(((bf16[4,32,1024]{2,1,0:T(8,128)(2,1)}), bf16[16,32,1024]{2,1,0:T(8,128)(2,1)}) %all-gather.3.cloned.1.call-update) | async-done | bytes 1048592 | tf_op jit(solution)/shard_map/all_gather | solution.py:164
  46.2 1.8 slice.77
  47.9 2.4 collective-permute-start
  50.4 27.6 %all-gather.5.cloned.1.call-done = bf16[16,32,1024]{2,1,0:T(8,128)(2,1)} async-done(((bf16[4,32,1024]{2,1,0:T(8,128)(2,1)}), bf16[16,32,1024]{2,1,0:T(8,128)(2,1)}) %all-gather.5.cloned.1.call-update) | async-done | bytes 1048592 | tf_op jit(solution)/shard_map/all_gather | solution.py:160
  78.0 1.7 convolution_convert_fusion.3
  79.7 2.4 collective-permute-start.4
  84.4 1.4 collective-permute-done.4
  86.5 4.2 collective-permute-start.5
  91.5 4.3 collective-permute-start.1
  96.1 2.2 collective-permute-done.1
  98.3 1.0 fusion.9
  100.5 1.2 reshape_reshape_squeeze.10
  103.3 1.2 fusion.57
  104.5 1.2 reshape_reshape_squeeze.11
  106.7 3.0 convolution_convert_fusion.2
  109.7 1.7 copy.46
  111.4 1.0 reshape.236
  113.3 2.5 collective-permute-start.2
  115.8 1.7 pad_maximum_fusion.2
  117.5 1.2 reshape_reshape.3
  120.9 4.4 collective-permute-start.3
  125.4 2.9 convolution_convert_fusion.1
  128.3 1.7 copy.55
  130.0 1.0 stack_reshape.11
  131.1 2.8 convolution_bitcast_fusion
  134.2 1.9 multiply_reduce_fusion
  136.4 1.2 fusion.16
  137.6 1.3 copy.53
  138.9 1.5 copy.54
  140.4 2.2 stack_reshape.10
  144.4 6.4 collective-permute-start.6
  150.8 7.1 collective-permute-done.6
  157.9 2.4 collective-permute-start.7
  160.3 7.9 %collective-permute-done.7 = bf16[16,4,3,256]{3,1,2,0:T(4,128)(2,1)S(1)} collective-permute-done((bf16[16,4,3,256]{3,1,2,0:T(4,128)(2,1)S(1)}, bf16[16,4,3,256]{3,1,2,0:T(4,128)(2,1)S(1)}, u32[]{:S(2)}, u32[]{:S(2)}) %collective-permute-start.7) | collective-permute-done | bytes 98336 | tf_op jit(solution)/shard_map/ppermute | solution.py:17
  168.2 2.0 bitcast_convert_fusion
  170.3 1.5 convolution_convert_fusion
  172.0 1.4 fusion.18
  173.4 266.7 %psum.7 = f32[225,4]{0,1:T(4,128)S(1)} all-reduce(f32[225,4]{0,1:T(4,128)S(1)} %fusion.18), channel_id=1, replica_groups=mesh['row'=32,'col'=4,'head'=4] {'row','col'}, use_global_device_ids=true, to_apply=%region_11.12 | all-reduce | flops 900 | bytes 7200 | tf_op jit(solution)/shard_map/psum | solution.py:200
  440.7 237.8 %reduce-scatter.8.cloned.1.call-done = f32[256,8]{0,1:T(8,128)} async-done(((f32[256,1024]{0,1:T(8,128)}), f32[256,8]{0,1:T(8,128)}) %reduce-scatter.8.cloned.1.call-update) | async-done | bytes 8208 | tf_op jit(solution)/shard_map/reduce_scatter | solution.py:198
  678.5 1.3 broadcast_multiply_fusion
  679.8 34.0 %reduce-scatter.6.cloned.1.call-done = bf16[4,32,1024]{2,1,0:T(8,128)(2,1)} async-done(((bf16[16,32,1024]{2,1,0:T(8,128)(2,1)}), bf16[4,32,1024]{2,1,0:T(8,128)(2,1)}) %reduce-scatter.6.cloned.1.call-update) | async-done | bytes 262160 | tf_op jit(solution)/shard_map/reduce_scatter | solution.py:87
  713.8 1.2 fusion.40
  715.0 30.1 %reduce-scatter.4.cloned.1.call-done = bf16[4,32,1024]{2,1,0:T(8,128)(2,1)} async-done(((bf16[16,32,1024]{2,1,0:T(8,128)(2,1)}), bf16[4,32,1024]{2,1,0:T(8,128)(2,1)}) %reduce-scatter.4.cloned.1.call-update) | async-done | bytes 262160 | tf_op jit(solution)/shard_map/reduce_scatter | solution.py:87
  745.1 2.1 fusion.35
  (107 shorter events, 16.3 us)
Async XLA Ops:
  7.2 91.1 %copy-start = (bf16[1024,3,256]{2,0,1:T(8,128)(2,1)S(1)}, bf16[1024,3,256]{2,0,1:T(8,128)(2,1)}, u32[]{:S(2)}) copy-start(bf16[1024,3,256]{2,0,1:T(8,128)(2,1)} %param.10) | copy-start | bytes 4718596
  7.2 5.9 copy-start.21
  7.2 6.8 copy-start.22
  7.2 38.9 %all-gather.3.cloned.1.call-start = ((), (), s32[]{:S(2)}) async-start(), calls=%async_computation.3 | async-start | bytes 1310720 | tf_op jit(solution)/shard_map/all_gather | solution.py:164
  8.4 1.3 copy-start.14
  8.4 69.5 %copy-start.8 = (bf16[256,1024]{1,0:T(8,128)(2,1)S(1)}, bf16[256,1024]{1,0:T(8,128)(2,1)}, u32[]{:S(2)}) copy-start(bf16[256,1024]{1,0:T(8,128)(2,1)} %param.11) | copy-start | bytes 1572868
  9.7 0.5 copy-start.17
  12.1 65.8 %all-gather.5.cloned.1.call-start = ((), (), s32[]{:S(2)}) async-start(), calls=%async_computation.5 | async-start | bytes 1310720 | tf_op jit(solution)/shard_map/all_gather | solution.py:160
  12.9 665.6 %reduce-scatter.8.cloned.1.call-start = ((), (), s32[]{:S(2)}) async-start(), calls=%async_computation.7 | async-start | bytes 1056768 | tf_op jit(solution)/shard_map/reduce_scatter | solution.py:198
  13.4 0.6 copy-start.19
  46.1 38.2 %copy-start.6 = (bf16[16,32,1024]{2,1,0:T(8,128)(2,1)S(1)}, bf16[16,32,1024]{2,1,0:T(8,128)(2,1)}, u32[]{:S(2)}) copy-start(bf16[16,32,1024]{2,1,0:T(8,128)(2,1)} %all-gather.3.cloned.1.call-done) | copy-start | bytes 3145732
  47.9 43.5 %collective-permute-start = (bf16[4,32,1024]{2,1,0:T(8,128)(2,1)}, bf16[4,32,1024]{2,1,0:T(8,128)(2,1)S(1)}, u32[]{:S(2)}, u32[]{:S(2)}) collective-permute-start(bf16[4,32,1024]{2,1,0:T(8,128)(2,1)} %slice.77), channel_id=1, source_target_pairs={{0,496},{16,0},{32,16},{48,32},{64,48},{80,64},{96,80},{112,96},{1... | collective-permute-start | bytes 786440 | tf_op jit(solution)/shard_map/ppermute | solution.py:17
  79.7 2.5 copy-start.11
  79.7 6.2 collective-permute-start.4
  86.5 29.3 %collective-permute-start.5 = (bf16[16,4,256]{2,1,0:T(4,128)(2,1)}, bf16[16,4,256]{2,1,0:T(4,128)(2,1)}, u32[]{:S(2)}, u32[]{:S(2)}) collective-permute-start(bf16[16,4,256]{2,1,0:T(4,128)(2,1)} %pad_maximum_fusion.5), channel_id=1, source_target_pairs={{0,12},{4,0},{8,4},{12,8},{1,13},{5,1},{9,5},{13,9},{2,14},{6,2},{... | collective-permute-start | bytes 98312 | tf_op jit(solution)/shard_map/ppermute | solution.py:17
  91.5 6.8 collective-permute-start.1
  102.3 1.0 copy-start.3
  113.3 7.6 %collective-permute-start.2 = (bf16[4,32,256]{2,1,0:T(8,128)(2,1)S(1)}, bf16[4,32,256]{2,1,0:T(8,128)(2,1)S(1)}, u32[]{:S(2)}, u32[]{:S(2)}) collective-permute-start(bf16[4,32,256]{2,1,0:T(8,128)(2,1)S(1)} %slice.83), channel_id=1, source_target_pairs={{0,16},{16,32},{32,48},{48,64},{64,80},{80,96},{96,112},{112,128},... | collective-permute-start | bytes 196616 | tf_op jit(solution)/shard_map/ppermute | solution.py:17
  120.9 10.1 %collective-permute-start.3 = (bf16[16,4,256]{2,1,0:T(4,128)(2,1)S(1)}, bf16[16,4,256]{2,1,0:T(4,128)(2,1)S(1)}, u32[]{:S(2)}, u32[]{:S(2)}) collective-permute-start(bf16[16,4,256]{2,1,0:T(4,128)(2,1)S(1)} %pad_maximum_fusion.6), channel_id=1, source_target_pairs={{0,4},{4,8},{8,12},{12,0},{1,5},{5,9},{9,13},{13,1},{2,6},{6,10},{... | collective-permute-start | bytes 98312 | tf_op jit(solution)/shard_map/ppermute | solution.py:17
  131.1 3.1 copy-start.10
  131.1 2.8 copy-start.12
  133.9 579.8 %reduce-scatter.6.cloned.1.call-start = ((), (), s32[]{:S(2)}) async-start(), calls=%async_computation.6 | async-start | bytes 1310720 | tf_op jit(solution)/shard_map/reduce_scatter | solution.py:87
  134.2 1.9 copy-start.2
  142.9 1.4 copy-start.5
  143.2 1.1 copy-start.4
  144.4 13.5 %collective-permute-start.6 = (bf16[4,32,3,256]{3,1,2,0:T(8,128)(2,1)S(1)}, bf16[4,32,3,256]{3,1,2,0:T(8,128)(2,1)S(1)}, u32[]{:S(2)}, u32[]{:S(2)}) collective-permute-start(bf16[4,32,3,256]{3,1,2,0:T(8,128)(2,1)S(1)} %slice.89), channel_id=1, source_target_pairs={{0,16},{16,32},{32,48},{48,64},{64,80},{80,96},{96,112},{112,128},... | collective-permute-start | bytes 589832 | tf_op jit(solution)/shard_map/ppermute | solution.py:17
  157.9 12.4 %copy-start.9 = (bf16[256,1024]{1,0:T(8,128)(2,1)S(1)}, bf16[256,1024]{1,0:T(8,128)(2,1)}, u32[]{:S(2)}) copy-start(bf16[256,1024]{1,0:T(8,128)(2,1)} %param.11) | copy-start | bytes 1572868
  157.9 12.4 %copy-start.13 = (bf16[16,4,256]{2,1,0:T(4,128)(2,1)S(1)}, bf16[16,4,256]{2,1,0:T(4,128)(2,1)}, u32[]{:S(2)}) copy-start(bf16[16,4,256]{2,1,0:T(4,128)(2,1)} %copy-done.12) | copy-start | bytes 98308
  157.9 10.3 %collective-permute-start.7 = (bf16[16,4,3,256]{3,1,2,0:T(4,128)(2,1)S(1)}, bf16[16,4,3,256]{3,1,2,0:T(4,128)(2,1)S(1)}, u32[]{:S(2)}, u32[]{:S(2)}) collective-permute-start(bf16[16,4,3,256]{3,1,2,0:T(4,128)(2,1)S(1)} %pad_maximum_fusion.4), channel_id=1, source_target_pairs={{0,4},{4,8},{8,12},{12,0},{1,5},{5,9},{9,13},{13,1},{2,6},{6,10},{... | collective-permute-start | bytes 294920 | tf_op jit(solution)/shard_map/ppermute | solution.py:17
  170.3 1.7 copy-start.20
  170.3 574.9 %reduce-scatter.4.cloned.1.call-start = ((), (), s32[]{:S(2)}) async-start(), calls=%async_computation.4 | async-start | bytes 1310720 | tf_op jit(solution)/shard_map/reduce_scatter | solution.py:87
  171.8 542.0 %copy-start.1 = (bf16[4,32,1024]{2,1,0:T(8,128)(2,1)S(1)}, bf16[4,32,1024]{2,1,0:T(8,128)(2,1)}, u32[]{:S(2)}) copy-start(bf16[4,32,1024]{2,1,0:T(8,128)(2,1)} %param.7) | copy-start | bytes 786436
  171.8 542.0 %copy-start.15 = (f32[4,32]{1,0:T(4,128)S(1)}, f32[4,32]{1,0:T(4,128)}, u32[]{:S(2)}) copy-start(f32[4,32]{1,0:T(4,128)} %copy-done.14) | copy-start | bytes 1540
  171.8 542.0 %copy-start.16 = (f32[1024]{0:T(1024)S(1)}, f32[1024]{0:T(1024)}, u32[]{:S(2)}) copy-start(f32[1024]{0:T(1024)} %param.9) | copy-start | bytes 12292
  171.8 542.0 %copy-start.18 = (f32[4,32]{1,0:T(4,128)S(1)}, f32[4,32]{1,0:T(4,128)}, u32[]{:S(2)}) copy-start(f32[4,32]{1,0:T(4,128)} %copy-done.17) | copy-start | bytes 1540
  171.8 573.3 %copy-start.7 = (bf16[4,32,1024]{2,1,0:T(8,128)(2,1)S(1)}, bf16[4,32,1024]{2,1,0:T(8,128)(2,1)}, u32[]{:S(2)}) copy-start(bf16[4,32,1024]{2,1,0:T(8,128)(2,1)} %param.13) | copy-start | bytes 786436
Sparse Core Ops, SparseCore 0:
  12.3 33.8 all-gather.2
  48.2 29.6 all-gather.4
  134.0 544.4 reduce-scatter.7
  681.4 32.2 reduce-scatter.5
  716.4 28.6 reduce-scatter.3
where the time goes:
time: 755 us; the launch traced here: 754 us
  waiting for transfers between devices  378 us (50%)
  blocking collectives  267 us (35%)
  starting transfers between devices  29.4 us (4%)
  local copies, waits for them, and re-layouts  26.9 us (4%)
  matrix products  23.6 us (3%)
  other arithmetic  14.9 us (2%)
  between operations  14.4 us (2%)
    psum x1, blocking collectives, on_device(): table_grad = lax.psum(tgrad, ('row', 'col')) * (WIN * scale)  267 us
    reduce_scatter x1, waiting for transfers between devices, on_device(): lax.psum_scatter(weight_term, ('row', 'col'), scatter_dimension=1, tiled=...  238 us
    reduce_scatter x2, waiting for transfers between devices, head_sum(): lax.psum_scatter(term_fn(jnp.int32(0), lax.axis_size('head') * part_rows)...  64.1 us
    ppermute x8, starting transfers between devices, passed_along(): return lax.ppermute(value, axis, pairs)  29 us
    all_gather x1, waiting for transfers between devices, on_device(): source = lax.all_gather(normalized_tokens, 'head', axis=0, tiled=True)  28.7 us
    all_gather x1, waiting for transfers between devices, on_device(): grad_tile = lax.all_gather(cotangent, 'head', axis=0, tiled=True)  27.6 us
    ppermute x8, waiting for transfers between devices, passed_along(): return lax.ppermute(value, axis, pairs)  19 us
  transfers between devices with their start and end apart: 13, of which 10 were waited for; matrix products, arithmetic and copies ran while one was open for 7% of the time, Pallas kernels for 0%

commit v1 on v0

--- a/solution.py
+++ b/solution.py
@@ -197,7 +197,7 @@
     proj_grad = (
         lax.psum_scatter(weight_term, ("row", "col"), scatter_dimension=1, tiled=True) * scale
     )
-    table_grad = lax.psum(tgrad, ("row", "col")) * (WIN * scale)
+    table_grad = lax.psum(lax.psum(tgrad, "col"), "row") * (WIN * scale)
     scaled_tokens = norm_grad * gain
     token_gradient = cotangent.astype(jnp.float32) + inverse_deviation * (
         scaled_tokens

time: 755 us -> 755 us (level)
  blocking collectives: 267 us -> 90 us
  waiting for transfers between devices: 378 us -> 555 us
    psum x1 -> x2, blocking collectives: 267 us -> 90 us  [on_device(): table_grad = lax.psum(lax.psum(tgrad, 'col'), 'row') * (WIN * scale)]
    reduce_scatter x1, waiting for transfers between devices: 238 us -> 414 us  [on_device(): lax.psum_scatter(weight_term, ('row', 'col'), scatter_dimension=1, tiled=...]
where the time goes in v1:
time: 755 us; the launch traced here: 754 us
  waiting for transfers between devices  555 us (74%)
  blocking collectives  90 us (12%)
  starting transfers between devices  29.4 us (4%)
  local copies, waits for them, and re-layouts  26.9 us (4%)
  matrix products  23.5 us (3%)
  other arithmetic  14.9 us (2%)
  between operations  14.4 us (2%)
    reduce_scatter x1, waiting for transfers between devices, on_device(): lax.psum_scatter(weight_term, ('row', 'col'), scatter_dimension=1, tiled=...  414 us
    psum x2, blocking collectives, on_device(): table_grad = lax.psum(lax.psum(tgrad, 'col'), 'row') * (WIN * scale)  90 us
    reduce_scatter x2, waiting for transfers between devices, head_sum(): lax.psum_scatter(term_fn(jnp.int32(0), lax.axis_size('head') * part_rows)...  64.8 us
    ppermute x8, starting transfers between devices, passed_along(): return lax.ppermute(value, axis, pairs)  29 us
    all_gather x1, waiting for transfers between devices, on_device(): source = lax.all_gather(normalized_tokens, 'head', axis=0, tiled=True)  28.7 us
    all_gather x1, waiting for transfers between devices, on_device(): grad_tile = lax.all_gather(cotangent, 'head', axis=0, tiled=True)  27.6 us
    ppermute x8, waiting for transfers between devices, passed_along(): return lax.ppermute(value, axis, pairs)  19 us
  transfers between devices with their start and end apart: 13, of which 10 were waited for; matrix products, arithmetic and copies ran while one was open for 7% of the time, Pallas kernels for 0%

profile of v1, /device:TPU:8, one launch (start us, length us, event | category | flops | bytes accessed | tf_op | source)
XLA Modules:
  0.0 753.7 jit_solution(17927255244606524388)
XLA Ops:
  7.2 1.2 convert_reduce_fusion
  8.5 1.2 fusion.36
  10.3 1.9 fusion.30
  14.1 3.4 fusion.17
  17.5 28.7 %all-gather.3.cloned.1.call-done = bf16[16,32,1024]{2,1,0:T(8,128)(2,1)} async-done(((bf16[4,32,1024]{2,1,0:T(8,128)(2,1)}), bf16[16,32,1024]{2,1,0:T(8,128)(2,1)}) %all-gather.3.cloned.1.call-update) | async-done | bytes 1048592 | tf_op jit(solution)/shard_map/all_gather | solution.py:164
  46.2 1.8 slice.77
  48.0 2.4 collective-permute-start
  50.4 27.6 %all-gather.5.cloned.1.call-done = bf16[16,32,1024]{2,1,0:T(8,128)(2,1)} async-done(((bf16[4,32,1024]{2,1,0:T(8,128)(2,1)}), bf16[16,32,1024]{2,1,0:T(8,128)(2,1)}) %all-gather.5.cloned.1.call-update) | async-done | bytes 1048592 | tf_op jit(solution)/shard_map/all_gather | solution.py:160
  78.0 1.7 convolution_convert_fusion.3
  79.7 2.4 collective-permute-start.4
  84.4 1.4 collective-permute-done.4
  86.5 4.2 collective-permute-start.5
  91.5 4.3 collective-permute-start.1
  96.1 2.2 collective-permute-done.1
  100.6 1.2 reshape_reshape_squeeze.10
  103.3 1.3 fusion.57
  104.6 1.2 reshape_reshape_squeeze.11
  106.8 2.9 convolution_convert_fusion.2
  109.7 1.7 copy.46
  111.4 1.0 reshape.236
  113.3 2.5 collective-permute-start.2
  115.8 1.7 pad_maximum_fusion.2
  117.5 1.2 reshape_reshape.3
  120.9 4.5 collective-permute-start.3
  125.4 2.9 convolution_convert_fusion.1
  128.3 1.7 copy.55
  130.0 1.0 stack_reshape.11
  131.1 2.8 convolution_bitcast_fusion
  134.2 1.9 multiply_reduce_fusion
  136.4 1.3 fusion.16
  137.7 1.3 copy.53
  139.0 1.5 copy.54
  140.5 2.2 stack_reshape.10
  144.4 6.3 collective-permute-start.6
  150.8 7.1 collective-permute-done.6
  158.0 2.4 collective-permute-start.7
  160.3 7.9 %collective-permute-done.7 = bf16[16,4,3,256]{3,1,2,0:T(4,128)(2,1)S(1)} collective-permute-done((bf16[16,4,3,256]{3,1,2,0:T(4,128)(2,1)S(1)}, bf16[16,4,3,256]{3,1,2,0:T(4,128)(2,1)S(1)}, u32[]{:S(2)}, u32[]{:S(2)}) %collective-permute-start.7) | collective-permute-done | bytes 98336 | tf_op jit(solution)/shard_map/ppermute | solution.py:17
  168.3 2.0 bitcast_convert_fusion
  170.4 1.5 convolution_convert_fusion
  172.0 1.4 fusion.18
  173.4 9.6 %psum.14 = f32[225,4]{0,1:T(4,128)S(1)} all-reduce(f32[225,4]{0,1:T(4,128)S(1)} %fusion.18), channel_id=1, replica_groups=mesh['row'=32,'col'=4,'head'=4] {'col'}, use_global_device_ids=true, to_apply=%region_11.12 | all-reduce | flops 900 | bytes 7200 | tf_op jit(solution)/shard_map/psum | solution.py:200
  183.0 80.4 %psum.15 = f32[225,4]{0,1:T(4,128)S(1)} all-reduce(f32[225,4]{0,1:T(4,128)S(1)} %psum.14), channel_id=1, replica_groups=mesh['row'=32,'col'=4,'head'=4] {'row'}, use_global_device_ids=true, to_apply=%region_12.13 | all-reduce | flops 900 | bytes 7200 | tf_op jit(solution)/shard_map/psum | solution.py:200
  264.0 413.7 %reduce-scatter.8.cloned.1.call-done = f32[256,8]{0,1:T(8,128)} async-done(((f32[256,1024]{0,1:T(8,128)}), f32[256,8]{0,1:T(8,128)}) %reduce-scatter.8.cloned.1.call-update) | async-done | bytes 8208 | tf_op jit(solution)/shard_map/reduce_scatter | solution.py:198
  677.7 1.3 broadcast_multiply_fusion
  679.0 34.7 %reduce-scatter.6.cloned.1.call-done = bf16[4,32,1024]{2,1,0:T(8,128)(2,1)} async-done(((bf16[16,32,1024]{2,1,0:T(8,128)(2,1)}), bf16[4,32,1024]{2,1,0:T(8,128)(2,1)}) %reduce-scatter.6.cloned.1.call-update) | async-done | bytes 262160 | tf_op jit(solution)/shard_map/reduce_scatter | solution.py:87
  713.8 1.2 fusion.40
  715.0 30.1 %reduce-scatter.4.cloned.1.call-done = bf16[4,32,1024]{2,1,0:T(8,128)(2,1)} async-done(((bf16[16,32,1024]{2,1,0:T(8,128)(2,1)}), bf16[4,32,1024]{2,1,0:T(8,128)(2,1)}) %reduce-scatter.4.cloned.1.call-update) | async-done | bytes 262160 | tf_op jit(solution)/shard_map/reduce_scatter | solution.py:87
  745.1 2.1 fusion.35
  (108 shorter events, 17.3 us)
Async XLA Ops:
  7.2 91.2 %copy-start = (bf16[1024,3,256]{2,0,1:T(8,128)(2,1)S(1)}, bf16[1024,3,256]{2,0,1:T(8,128)(2,1)}, u32[]{:S(2)}) copy-start(bf16[1024,3,256]{2,0,1:T(8,128)(2,1)} %param.10) | copy-start | bytes 4718596
  7.2 6.0 copy-start.21
  7.2 6.9 copy-start.22
  7.2 39.0 %all-gather.3.cloned.1.call-start = ((), (), s32[]{:S(2)}) async-start(), calls=%async_computation.3 | async-start | bytes 1310720 | tf_op jit(solution)/shard_map/all_gather | solution.py:164
  8.4 1.3 copy-start.14
  8.4 69.6 %copy-start.8 = (bf16[256,1024]{1,0:T(8,128)(2,1)S(1)}, bf16[256,1024]{1,0:T(8,128)(2,1)}, u32[]{:S(2)}) copy-start(bf16[256,1024]{1,0:T(8,128)(2,1)} %param.11) | copy-start | bytes 1572868
  9.7 0.6 copy-start.17
  12.2 65.8 %all-gather.5.cloned.1.call-start = ((), (), s32[]{:S(2)}) async-start(), calls=%async_computation.5 | async-start | bytes 1310720 | tf_op jit(solution)/shard_map/all_gather | solution.py:160
  12.9 664.8 %reduce-scatter.8.cloned.1.call-start = ((), (), s32[]{:S(2)}) async-start(), calls=%async_computation.7 | async-start | bytes 1056768 | tf_op jit(solution)/shard_map/reduce_scatter | solution.py:198
  13.5 0.6 copy-start.19
  46.2 38.2 %copy-start.6 = (bf16[16,32,1024]{2,1,0:T(8,128)(2,1)S(1)}, bf16[16,32,1024]{2,1,0:T(8,128)(2,1)}, u32[]{:S(2)}) copy-start(bf16[16,32,1024]{2,1,0:T(8,128)(2,1)} %all-gather.3.cloned.1.call-done) | copy-start | bytes 3145732
  48.0 43.5 %collective-permute-start = (bf16[4,32,1024]{2,1,0:T(8,128)(2,1)}, bf16[4,32,1024]{2,1,0:T(8,128)(2,1)S(1)}, u32[]{:S(2)}, u32[]{:S(2)}) collective-permute-start(bf16[4,32,1024]{2,1,0:T(8,128)(2,1)} %slice.77), channel_id=1, source_target_pairs={{0,496},{16,0},{32,16},{48,32},{64,48},{80,64},{96,80},{112,96},{1... | collective-permute-start | bytes 786440 | tf_op jit(solution)/shard_map/ppermute | solution.py:17
  79.7 2.5 copy-start.11
  79.7 6.2 collective-permute-start.4
  86.5 29.3 %collective-permute-start.5 = (bf16[16,4,256]{2,1,0:T(4,128)(2,1)}, bf16[16,4,256]{2,1,0:T(4,128)(2,1)}, u32[]{:S(2)}, u32[]{:S(2)}) collective-permute-start(bf16[16,4,256]{2,1,0:T(4,128)(2,1)} %pad_maximum_fusion.5), channel_id=1, source_target_pairs={{0,12},{4,0},{8,4},{12,8},{1,13},{5,1},{9,5},{13,9},{2,14},{6,2},{... | collective-permute-start | bytes 98312 | tf_op jit(solution)/shard_map/ppermute | solution.py:17
  91.5 6.8 collective-permute-start.1
  102.3 1.0 copy-start.3
  113.3 7.6 %collective-permute-start.2 = (bf16[4,32,256]{2,1,0:T(8,128)(2,1)S(1)}, bf16[4,32,256]{2,1,0:T(8,128)(2,1)S(1)}, u32[]{:S(2)}, u32[]{:S(2)}) collective-permute-start(bf16[4,32,256]{2,1,0:T(8,128)(2,1)S(1)} %slice.83), channel_id=1, source_target_pairs={{0,16},{16,32},{32,48},{48,64},{64,80},{80,96},{96,112},{112,128},... | collective-permute-start | bytes 196616 | tf_op jit(solution)/shard_map/ppermute | solution.py:17
  120.9 10.1 %collective-permute-start.3 = (bf16[16,4,256]{2,1,0:T(4,128)(2,1)S(1)}, bf16[16,4,256]{2,1,0:T(4,128)(2,1)S(1)}, u32[]{:S(2)}, u32[]{:S(2)}) collective-permute-start(bf16[16,4,256]{2,1,0:T(4,128)(2,1)S(1)} %pad_maximum_fusion.6), channel_id=1, source_target_pairs={{0,4},{4,8},{8,12},{12,0},{1,5},{5,9},{9,13},{13,1},{2,6},{6,10},{... | collective-permute-start | bytes 98312 | tf_op jit(solution)/shard_map/ppermute | solution.py:17
  131.1 3.1 copy-start.10
  131.1 2.8 copy-start.12
  133.9 579.8 %reduce-scatter.6.cloned.1.call-start = ((), (), s32[]{:S(2)}) async-start(), calls=%async_computation.6 | async-start | bytes 1310720 | tf_op jit(solution)/shard_map/reduce_scatter | solution.py:87
  134.2 1.9 copy-start.2
  143.0 1.4 copy-start.5
  143.3 1.1 copy-start.4
  144.4 13.5 %collective-permute-start.6 = (bf16[4,32,3,256]{3,1,2,0:T(8,128)(2,1)S(1)}, bf16[4,32,3,256]{3,1,2,0:T(8,128)(2,1)S(1)}, u32[]{:S(2)}, u32[]{:S(2)}) collective-permute-start(bf16[4,32,3,256]{3,1,2,0:T(8,128)(2,1)S(1)} %slice.89), channel_id=1, source_target_pairs={{0,16},{16,32},{32,48},{48,64},{64,80},{80,96},{96,112},{112,128},... | collective-permute-start | bytes 589832 | tf_op jit(solution)/shard_map/ppermute | solution.py:17
  158.0 12.4 %copy-start.9 = (bf16[256,1024]{1,0:T(8,128)(2,1)S(1)}, bf16[256,1024]{1,0:T(8,128)(2,1)}, u32[]{:S(2)}) copy-start(bf16[256,1024]{1,0:T(8,128)(2,1)} %param.11) | copy-start | bytes 1572868
  158.0 12.4 %copy-start.13 = (bf16[16,4,256]{2,1,0:T(4,128)(2,1)S(1)}, bf16[16,4,256]{2,1,0:T(4,128)(2,1)}, u32[]{:S(2)}) copy-start(bf16[16,4,256]{2,1,0:T(4,128)(2,1)} %copy-done.12) | copy-start | bytes 98308
  158.0 10.3 %collective-permute-start.7 = (bf16[16,4,3,256]{3,1,2,0:T(4,128)(2,1)S(1)}, bf16[16,4,3,256]{3,1,2,0:T(4,128)(2,1)S(1)}, u32[]{:S(2)}, u32[]{:S(2)}) collective-permute-start(bf16[16,4,3,256]{3,1,2,0:T(4,128)(2,1)S(1)} %pad_maximum_fusion.4), channel_id=1, source_target_pairs={{0,4},{4,8},{8,12},{12,0},{1,5},{5,9},{9,13},{13,1},{2,6},{6,10},{... | collective-permute-start | bytes 294920 | tf_op jit(solution)/shard_map/ppermute | solution.py:17
  170.3 1.7 copy-start.20
  170.3 574.8 %reduce-scatter.4.cloned.1.call-start = ((), (), s32[]{:S(2)}) async-start(), calls=%async_computation.4 | async-start | bytes 1310720 | tf_op jit(solution)/shard_map/reduce_scatter | solution.py:87
  171.8 541.9 %copy-start.1 = (bf16[4,32,1024]{2,1,0:T(8,128)(2,1)S(1)}, bf16[4,32,1024]{2,1,0:T(8,128)(2,1)}, u32[]{:S(2)}) copy-start(bf16[4,32,1024]{2,1,0:T(8,128)(2,1)} %param.7) | copy-start | bytes 786436
  171.8 541.9 %copy-start.15 = (f32[4,32]{1,0:T(4,128)S(1)}, f32[4,32]{1,0:T(4,128)}, u32[]{:S(2)}) copy-start(f32[4,32]{1,0:T(4,128)} %copy-done.14) | copy-start | bytes 1540
  171.8 541.9 %copy-start.16 = (f32[1024]{0:T(1024)S(1)}, f32[1024]{0:T(1024)}, u32[]{:S(2)}) copy-start(f32[1024]{0:T(1024)} %param.9) | copy-start | bytes 12292
  171.8 541.9 %copy-start.18 = (f32[4,32]{1,0:T(4,128)S(1)}, f32[4,32]{1,0:T(4,128)}, u32[]{:S(2)}) copy-start(f32[4,32]{1,0:T(4,128)} %copy-done.17) | copy-start | bytes 1540
  171.9 573.3 %copy-start.7 = (bf16[4,32,1024]{2,1,0:T(8,128)(2,1)S(1)}, bf16[4,32,1024]{2,1,0:T(8,128)(2,1)}, u32[]{:S(2)}) copy-start(bf16[4,32,1024]{2,1,0:T(8,128)(2,1)} %param.13) | copy-start | bytes 786436
Sparse Core Ops, SparseCore 0:
  12.3 33.8 all-gather.2
  48.3 29.6 all-gather.4
  134.0 543.6 reduce-scatter.7
  680.7 33.0 reduce-scatter.5
  716.5 28.6 reduce-scatter.3
